TPU v7x, 32 devices: a whole 2x2x4 slice. The times are simulated.
32 devices in a mesh: groups: 2 (over y), tile: 4 (over z), tracer: 4 (over x, core).
Axes of the slice: x: 2, y: 2, z: 4, core: 2. Of those that a mesh axis runs over, the one named last changes fastest.
Arguments:
- species_amounts: float32 [64, 32, 128, 128], P(('groups', 'tracer'), None, 'tile'), parts along dimension 0, may hold values from 0.2 to 2
- face_currents: float32 [2, 64, 128, 128], P(None, 'groups', 'tile'), parts along dimension 1, may hold values from -1 to 1
- thermal_anomaly: float32 [64, 128, 128], P(('groups', 'tracer'), 'tile'), parts along dimension 0, may hold values from -4 to 4
- layer_total_per_profile: int32 [256, 128], P(('groups', 'tile')), parts along dimension 0, may hold values from 0 to 32
- consumed_species: int32 [32], replicated, may hold values from 0 to 31, each once
- attenuation_factor: float32 [32], replicated, may hold values from 0.009375 to 0.09375
- intake_speedup: float32 [32], replicated, may hold values from 0.3 to 3
- incoming_sunshine: float32 [256, 128], P(('groups', 'tile')), parts along dimension 0, may hold values from 0.5 to 2
Outputs:
- tracers_out: float32 [64, 32, 128, 128], P('groups', 'tracer', 'tile'), parts along dimension 0
- velocity_out: float32 [2, 64, 128, 128], P(None, ('groups', 'tracer'), 'tile'), parts along dimension 1
- temperature_out: float32 [64, 128, 128], P(('groups', 'tracer'), 'tile'), parts along dimension 0
There are 2 independent parts, one for each index of `groups`. A program takes and returns all parts, laid end to end along the dimension named above; an argument that names none is the same for every part. Nothing has to cross between parts.
Inputs may be any that keep to these rules, and one draw needn't show every extreme that they name: Levels 0 to layer_total_per_profile - 1 of a column are sea, deeper levels are land; 0 marks a land column. `consumed_species`: A permutation of the 32 tracers.
All inputs are finite; a program needn't handle non-finite values.
Results may differ from a plain program's by a relative error of at most 0.0003.
Values sent between devices are 32-bit elements; how exact they have to be, the bound alone decides.
No kernel may reach another device: no remote copies, remote signals or barrier semaphores. Data moves between devices by JAX's collectives and lax.ppermute only.
A program may use at most 64 MiB of HBM per device.

v0:
```python
import jax
import jax.numpy as jnp
from jax import lax
from jax.sharding import PartitionSpec as P

DEPTH_LAYERS = 32


sub_step = 0.45
step_duration = 0.2
gravity = 0.5
viscosity = 0.2
coriolis_base = 0.5
beta_plane = 0.5
spreading_coefficient = 0.2
water_clear = 0.05
column_optical = 3.0
warming_coefficient = 5.0
light_half = 0.3
nutrient_half = 0.5


def padded(block, sides, width):
    for axis, dim in sides:
        count = lax.axis_size(axis)
        forward = [(i, i + 1) for i in range(count - 1)]
        forward.append((count - 1, 0))
        backward = [(target, source) for source, target in forward]
        low = lax.ppermute(
            lax.slice_in_dim(block, block.shape[dim] - width, None, axis=dim), axis, forward
        )
        high = lax.ppermute(lax.slice_in_dim(block, 0, width, axis=dim), axis, backward)
        block = jnp.concatenate([low, block, high], axis=dim)
    return block


def prefix(part, axis, combine, identity):
    place = lax.axis_index(axis)
    gathered = lax.all_gather(part, axis)
    state = jnp.zeros_like(part) + jnp.asarray(identity, part.dtype)

    def one(hop, state):
        return combine(state, lax.dynamic_index_in_dim(gathered, hop, 0, False))

    return lax.fori_loop(0, place, one, state)


def shift_south(values):
    return jnp.concatenate([jnp.zeros_like(values[..., :1]), values[..., :-1]], axis=-1)


def shift_north(values, offset=1):
    return jnp.concatenate([values[..., offset:], jnp.zeros_like(values[..., :offset])], axis=-1)


def wet_levels(depth_ext, first_level, level_count):
    levels = first_level + jnp.arange(level_count, dtype=jnp.int32)
    return (levels[:, None, None] < depth_ext[None]).astype(jnp.float32)


def limiter(left_slope, right_slope):
    smaller = jnp.minimum(jnp.abs(left_slope), jnp.abs(right_slope))
    return jnp.where(left_slope * right_slope > 0.0, jnp.sign(left_slope) * smaller, 0.0)


def face_flux(behind, centre, forward, beyond, speed):
    positive = speed * (centre + 0.5 * limiter(centre - behind, forward - centre))
    negative = speed * (forward - 0.5 * limiter(forward - centre, beyond - forward))
    return jnp.where(speed > 0.0, positive, negative)


def face_speeds(velocity_with_halo_border, wet_ext):
    east_speed = velocity_with_halo_border[0][:, :-1] * wet_ext[:, :-1] * wet_ext[:, 1:]
    north_speed = velocity_with_halo_border[1] * wet_ext * shift_north(wet_ext)
    return (east_speed, north_speed)


def flux_substep(extended, east_speed, north_speed):
    length = extended.shape[2]
    east_flux = face_flux(
        extended[:, :, 0 : length - 3],
        extended[:, :, 1 : length - 2],
        extended[:, :, 2 : length - 1],
        extended[:, :, 3:length],
        east_speed[:, 1 : length - 2],
    )
    middle = extended[:, :, 2 : length - 2]
    north_flux = face_flux(
        shift_south(middle),
        middle,
        shift_north(middle),
        shift_north(middle, 2),
        north_speed[:, 2 : length - 2],
    )
    spread = east_flux[:, :, 1:] - east_flux[:, :, :-1] + (north_flux - shift_south(north_flux))
    return middle - sub_step * spread


def advect(values, velocity_with_halo_border, wet_ext):
    east_speed, north_speed = face_speeds(velocity_with_halo_border, wet_ext)
    for repeat in range(2):
        extended = padded(values, (("tile", 2),), 2)
        values = flux_substep(extended, east_speed, north_speed)
    return values


def to_cells(values):
    return lax.all_to_all(values, "tracer", split_axis=1, concat_axis=0, tiled=True)


def laplacian(values):
    inner = values[:, 1:-1]
    return values[:, 2:] + values[:, :-2] + shift_north(inner) + shift_south(inner) - 4.0 * inner


def velocity_advance(flow_one, marine_mask_profile, thermal_profile_alone):
    east_vel = flow_one[0]
    north_vel = flow_one[1]
    ocean_profiles = east_vel.shape[1] - 2
    coriolis_y = (
        coriolis_base
        + beta_plane * jnp.arange(east_vel.shape[2], dtype=jnp.float32) / east_vel.shape[2]
    )
    centre_u = east_vel[:, 1 : ocean_profiles + 1]
    centre_v = north_vel[:, 1 : ocean_profiles + 1]
    v_bar = 0.25 * (
        centre_v + north_vel[:, 2:] + shift_south(centre_v) + shift_south(north_vel[:, 2:])
    )
    u_bar = 0.25 * (
        centre_u + east_vel[:, :-2] + shift_north(centre_u) + shift_north(east_vel[:, :-2])
    )
    marine_mask_interior = marine_mask_profile[:, 1 : ocean_profiles + 1]
    east_open = marine_mask_interior * marine_mask_profile[:, 2:]
    north_open = marine_mask_interior * shift_north(marine_mask_interior)
    heat_mid = thermal_profile_alone[:, 1 : ocean_profiles + 1]
    new_east = east_open * (
        centre_u
        + step_duration
        * (
            coriolis_y * v_bar
            - gravity * (thermal_profile_alone[:, 2:] - heat_mid)
            + viscosity * laplacian(east_vel)
        )
    )
    new_north = north_open * (
        centre_v
        + step_duration
        * (
            -coriolis_y * u_bar
            - gravity * (shift_north(heat_mid) - heat_mid)
            + viscosity * laplacian(north_vel)
        )
    )
    return (jnp.stack([new_east, new_north]), laplacian(thermal_profile_alone))


def optical_thickness(by_cells, attenuation_factor):
    summed = jnp.tensordot(
        attenuation_factor, jnp.abs(by_cells), axes=1, precision=lax.Precision.HIGHEST
    )
    return (water_clear + summed) * (column_optical / DEPTH_LAYERS)


def react(
    by_cells, optical, overhead, wet_mask, incoming_sunshine, intake_speedup, consumed_species
):
    depth_tau = overhead[None] + (jnp.cumsum(optical, axis=0) - optical)
    reaching = incoming_sunshine[None] * jnp.exp(-depth_tau)
    absorbed_part = 1.0 - jnp.exp(-optical)
    captured_radiance = reaching * absorbed_part * wet_mask
    mean_light = reaching * absorbed_part / optical
    light_limit = mean_light / (mean_light + light_half)
    pairing = (
        consumed_species[:, None] == jnp.arange(by_cells.shape[0], dtype=jnp.int32)[None]
    ).astype(jnp.float32)
    nutrient = jnp.tensordot(pairing, by_cells, axes=1, precision=lax.Precision.HIGHEST)
    uptake = (
        intake_speedup[:, None, None, None]
        * light_limit[None]
        * by_cells
        * nutrient
        / (nutrient_half + jnp.abs(nutrient))
    )
    consumed = jnp.tensordot(pairing.T, uptake, axes=1, precision=lax.Precision.HIGHEST)
    updated = by_cells + wet_mask[None] * (uptake - consumed)
    return (updated, captured_radiance)


def add_depths(earlier, later):
    return earlier + later


def on_device(
    species_amounts,
    face_currents,
    thermal_anomaly,
    layer_total_per_profile,
    consumed_species,
    attenuation_factor,
    intake_speedup,
    incoming_sunshine,
):
    layer_indices_here = thermal_anomaly.shape[0]
    ocean_profiles = thermal_anomaly.shape[1]
    first_level = lax.axis_index("tracer") * layer_indices_here
    margin = 2
    depth_ext = padded(layer_total_per_profile, (("tile", 0),), margin)
    flow_slice = lax.dynamic_slice_in_dim(face_currents, first_level, layer_indices_here, 1)
    velocity_with_halo_border = padded(flow_slice, (("tile", 2),), margin)
    wet_ext = wet_levels(depth_ext, first_level, layer_indices_here)
    by_cells = advect(to_cells(species_amounts), velocity_with_halo_border, wet_ext)
    thermal_profile_alone = padded(thermal_anomaly, (("tile", 1),), 1)
    flow_one = velocity_with_halo_border[:, :, margin - 1 : margin + ocean_profiles + 1]
    marine_mask_profile = wet_ext[:, margin - 1 : margin + ocean_profiles + 1]
    advanced_face_speeds, thermal_second_derivative = velocity_advance(
        flow_one, marine_mask_profile, thermal_profile_alone
    )
    marine_mask_interior = marine_mask_profile[:, 1:-1]
    optical = optical_thickness(by_cells, attenuation_factor)
    overhead = prefix(
        jnp.sum(optical, axis=0), "tracer", add_depths, jnp.zeros(optical.shape[1:], jnp.float32)
    )
    updated, captured_radiance = react(
        by_cells,
        optical,
        overhead,
        marine_mask_interior,
        incoming_sunshine,
        intake_speedup,
        consumed_species,
    )
    advanced_thermal_field = marine_mask_interior * (
        thermal_anomaly
        + step_duration * spreading_coefficient * thermal_second_derivative
        + warming_coefficient * captured_radiance
    )
    return (updated, advanced_face_speeds, advanced_thermal_field)


def solution(mesh):
    return jax.shard_map(
        on_device,
        mesh=mesh,
        in_specs=(
            P(("groups", "tracer"), None, "tile", None),
            P(None, "groups", "tile", None),
            P(("groups", "tracer"), "tile", None),
            P(("groups", "tile"), None),
            P(),
            P(),
            P(),
            P(("groups", "tile"), None),
        ),
        out_specs=(
            P("groups", "tracer", "tile", None),
            P(None, ("groups", "tracer"), "tile", None),
            P(("groups", "tracer"), "tile", None),
        ),
        check_vma=False,
    )
```

profile of v0, /device:TPU:1, one launch (start us, length us, event | category | flops | bytes accessed | tf_op | source)
XLA Modules:
  0.0 157.7 jit_solution(5242517074620127479)
XLA Ops:
  0.6 0.0 copy-start
  0.7 0.9 constant_dynamic-slice_fusion.1
  1.6 2.2 %collective-permute-start = (f32[2,8,2,128]{3,2,1,0:T(2,128)S(1)}, f32[2,8,2,128]{3,2,1,0:T(2,128)S(1)}, u32[]{:S(2)}, u32[]{:S(2)}) collective-permute-start(f32[2,8,2,128]{3,2,1,0:T(2,128)S(1)} %get-tuple-element.53), channel_id=1, source_target_pairs={{0,4},{4,8},{8,12},{12,0},{1,5},{5,9},{9,13},{13,1},{2,6},{6,10},{... | collective-permute-start | bytes 49160 | tf_op jit(solution)/shard_map/ppermute | solution.py:29
  3.7 2.1 %collective-permute-start.1 = (f32[2,8,2,128]{3,2,1,0:T(2,128)S(1)}, f32[2,8,2,128]{3,2,1,0:T(2,128)S(1)}, u32[]{:S(2)}, u32[]{:S(2)}) collective-permute-start(f32[2,8,2,128]{3,2,1,0:T(2,128)S(1)} %get-tuple-element.54), channel_id=1, source_target_pairs={{4,0},{8,4},{12,8},{0,12},{5,1},{9,5},{13,9},{1,13},{6,2},{10,6},{... | collective-permute-start | bytes 49160 | tf_op jit(solution)/shard_map/ppermute | solution.py:32
  5.8 0.7 fusion.83
  6.5 0.0 collective-permute-start.2
  6.5 3.3 %collective-permute-start.3 = (s32[2,128]{1,0:T(2,128)S(1)}, s32[2,128]{1,0:T(2,128)S(1)}, u32[]{:S(2)}, u32[]{:S(2)}) collective-permute-start(s32[2,128]{1,0:T(2,128)S(1)} %get-tuple-element.77), channel_id=1, source_target_pairs={{4,0},{8,4},{12,8},{0,12},{5,1},{9,5},{13,9},{1,13},{6,2},{10,6},{... | collective-permute-start | bytes 3080 | tf_op jit(solution)/shard_map/ppermute | solution.py:32
  9.8 4.8 %copy.14 = f32[8,32,32,128]{3,2,0,1:T(8,128)} copy(f32[8,32,32,128]{3,2,1,0:T(8,128)} %param.10) | data formatting | bytes 8388608 | tf_op args[0]
  14.6 6.5 %all-to-all-start = ((f32[8,32,32,128]{3,2,0,1:T(8,128)}), f32[8,32,32,128]{3,2,0,1:T(8,128)}, u32[]{:S(2)}, u32[]{:S(2)}) async-start(f32[8,32,32,128]{3,2,0,1:T(8,128)} %copy.14), calls=%async_computation | async-start | bytes 8388608 | tf_op jit(solution)/shard_map/all_to_all | solution.py:108
  21.1 0.0 copy-done.2
  21.1 0.1 collective-permute-start.8
  21.2 1.0 constant_dynamic-slice_fusion.2
  22.2 0.1 fusion.81
  22.3 0.0 collective-permute-done.2
  22.3 1.5 collective-permute-start.9
  23.8 0.0 collective-permute-done.3
  23.8 0.0 copy-done.3
  23.8 0.1 broadcast_compare_fusion.1
  23.9 0.1 slice.288
  24.0 0.1 slice.320
  24.2 0.0 collective-permute-done
  24.2 0.0 collective-permute-done.1
  24.3 0.2 fusion.78
  24.4 0.2 fusion.46
  24.6 0.0 collective-permute-done.8
  24.6 0.2 fusion.55
  24.8 0.7 pad_maximum_fusion.5
  25.6 0.1 broadcast_compare_fusion.2
  25.7 0.1 broadcast_compare_fusion
  25.8 42.6 %all-to-all-done = f32[8,32,32,128]{3,2,0,1:T(8,128)} async-done(((f32[8,32,32,128]{3,2,0,1:T(8,128)}), f32[8,32,32,128]{3,2,0,1:T(8,128)}, u32[]{:S(2)}, u32[]{:S(2)}) %all-to-all-start) | async-done | bytes 4194336 | tf_op jit(solution)/shard_map/all_to_all | solution.py:108
  68.4 4.6 %copy.28 = f32[8,4,8,32,128]{4,0,1,3,2:T(8,128)S(1)} copy(f32[8,4,8,32,128]{4,3,0,2,1:T(8,128)} %bitcast.1) | data formatting | bytes 8388608 | tf_op jit(solution)/shard_map/all_to_all | solution.py:108
  72.9 1.6 %fusion.76 = (f32[32,8,32,127]{3,0,2,1:T(8,128)S(1)}, f32[32,8,32,127]{3,0,2,1:T(8,128)S(1)}) fusion(f32[32,8,32,128]{3,0,2,1:T(8,128)S(1)} %bitcast.45), kind=kLoop, calls=%fused_computation.133 | loop fusion | bytes 16646144 | tf_op jit(solution)/shard_map/slice | solution.py:49
  74.6 1.1 slice.293
  75.8 0.1 collective-permute-start.4
  75.8 3.3 %collective-permute-start.5 = (f32[32,8,2,128]{3,0,2,1:T(8,128)S(1)}, f32[32,8,2,128]{3,0,2,1:T(8,128)S(1)}, u32[]{:S(2)}, u32[]{:S(2)}) collective-permute-start(f32[32,8,2,128]{3,0,2,1:T(8,128)S(1)} %get-tuple-element.52), channel_id=1, source_target_pairs={{4,0},{8,4},{12,8},{0,12},{5,1},{9,5},{13,9},{1,13},{6,2},{10,6},{... | collective-permute-start | bytes 786440 | tf_op jit(solution)/shard_map/ppermute | solution.py:32
  79.1 8.8 %multiply_select_fusion.3 = f32[32,8,32,128]{3,0,2,1:T(8,128)S(1)} fusion(f32[32,8,32,126]{3,0,2,1:T(8,128)S(1)} %slice.293, f32[32,8,32,127]{3,0,2,1:T(8,128)S(1)} %get-tuple-element.50, f32[32,8,32,127]{3,0,2,1:T(8,128)S(1)} %get-tuple-element.49, f32[8,32,128]{2,1,0:T(8,128)S(1)} %get-tuple-element.42, pred[8,32,128]{2,1,0:T(8,128)(4,1)S(1)} %get-tuple-element.41, ...), kind=kLoop, calls=%fused_computation.48 | loop fusion | flops 26214400 | bytes 21004288 | tf_op jit(solution)/shard_map/jit(_where)/select_n | solution.py:69
  87.9 0.0 collective-permute-done.4
  87.9 0.7 collective-permute-done.5
  88.6 5.6 %multiply_select_fusion.1 = f32[32,8,33,128]{3,0,2,1:T(8,128)S(1)} fusion(f32[32,8,2,128]{3,0,2,1:T(8,128)S(1)} %collective-permute-done.5, f32[32,8,32,128]{3,0,2,1:T(8,128)S(1)} %bitcast.48, f32[32,8,2,128]{3,0,2,1:T(8,128)S(1)} %collective-permute-done.4, f32[8,33,128]{2,1,0:T(8,128)S(1)} %get-tuple-element.44, pred[8,33,128]{2,1,0:T(8,128)(4,1)S(1)} %get-tuple-element.43), kind=kLoop, calls=%fused_computation.26 | loop fusion | flops 31358976 | bytes 9212928 | tf_op jit(solution)/shard_map/jit(_where)/select_n | solution.py:69
  94.1 5.6 %fusion.17 = f32[32,8,32,128]{3,0,2,1:T(8,128)S(1)} fusion(f32[32,8,33,128]{3,0,2,1:T(8,128)S(1)} %multiply_select_fusion.1, f32[32,8,32,128]{3,0,2,1:T(8,128)S(1)} %multiply_select_fusion.3, f32[32,8,32,127]{3,0,2,1:T(8,128)S(1)} %bitcast.50, f32[8,4,8,32,128]{4,3,0,2,1:T(8,128)} %bitcast.1), kind=kLoop, calls=%fused_computation.38 | loop fusion | flops 5242880 | bytes 25133056 | tf_op jit(solution)/shard_map/sub | solution.py:96
  99.7 1.5 fusion.74
  101.2 1.1 slice.305
  102.4 0.1 collective-permute-start.6
  102.5 3.3 %collective-permute-start.7 = (f32[32,8,2,128]{3,0,2,1:T(8,128)S(1)}, f32[32,8,2,128]{3,0,2,1:T(8,128)S(1)}, u32[]{:S(2)}, u32[]{:S(2)}) collective-permute-start(f32[32,8,2,128]{3,0,2,1:T(8,128)S(1)} %get-tuple-element.48), channel_id=1, source_target_pairs={{4,0},{8,4},{12,8},{0,12},{5,1},{9,5},{13,9},{1,13},{6,2},{10,6},{... | collective-permute-start | bytes 786440 | tf_op jit(solution)/shard_map/ppermute | solution.py:32
  105.7 7.5 %multiply_select_fusion.2 = f32[32,8,32,128]{3,0,2,1:T(8,128)} fusion(f32[32,8,32,126]{3,0,2,1:T(8,128)S(1)} %slice.305, f32[32,8,32,128]{3,0,2,1:T(8,128)S(1)} %fusion.17, f32[32,8,32,127]{3,0,2,1:T(8,128)S(1)} %get-tuple-element.46, f32[32,8,32,127]{3,0,2,1:T(8,128)S(1)} %get-tuple-element.45, f32[8,32,128]{2,1,0:T(8,128)S(1)} %get-tuple-element.42, ...), kind=kLoop, calls=%fused_computation.44 | loop fusion | flops 26214400 | bytes 21004288 | tf_op jit(solution)/shard_map/jit(_where)/select_n | solution.py:69
  113.2 0.0 collective-permute-done.6
  113.2 2.8 %collective-permute-done.7 = f32[32,8,2,128]{3,0,2,1:T(8,128)S(1)} collective-permute-done((f32[32,8,2,128]{3,0,2,1:T(8,128)S(1)}, f32[32,8,2,128]{3,0,2,1:T(8,128)S(1)}, u32[]{:S(2)}, u32[]{:S(2)}) %collective-permute-start.7) | collective-permute-done | bytes 262176 | tf_op jit(solution)/shard_map/ppermute | solution.py:32
  116.0 6.5 %multiply_select_fusion = f32[32,8,33,128]{3,0,2,1:T(8,128)} fusion(f32[32,8,2,128]{3,0,2,1:T(8,128)S(1)} %collective-permute-done.7, f32[32,8,32,128]{3,0,2,1:T(8,128)S(1)} %fusion.17, f32[32,8,2,128]{3,0,2,1:T(8,128)S(1)} %collective-permute-done.6, f32[8,33,128]{2,1,0:T(8,128)S(1)} %get-tuple-element.44, pred[8,33,128]{2,1,0:T(8,128)(4,1)S(1)} %get-tuple-element.43), kind=kLoop, calls=%fused_computation.21 | loop fusion | flops 31358976 | bytes 9212928 | tf_op jit(solution)/shard_map/jit(_where)/select_n | solution.py:69
  122.6 9.9 %fusion.14 = f32[32,8,32,128]{3,0,2,1:T(8,128)} fusion(f32[32,8,32,128]{3,0,2,1:T(8,128)S(1)} %fusion.17, f32[32,8,33,128]{3,0,2,1:T(8,128)} %multiply_select_fusion, f32[32,8,32,128]{3,0,2,1:T(8,128)} %multiply_select_fusion.2, f32[32,8,32,127]{3,0,2,1:T(8,128)} %bitcast.49), kind=kLoop, calls=%fused_computation.34 | loop fusion | flops 5242880 | bytes 25133056 | tf_op jit(solution)/shard_map/sub | solution.py:96
  132.5 0.0 copy-done
  132.5 4.5 %fusion.18 = f32[1,8,32,128]{3,0,2,1:T(1,128)S(1)} fusion(f32[32,8,32,128]{3,0,2,1:T(8,128)} %fusion.14, f32[32]{0:T(128)S(1)} %copy-done), kind=kOutput, calls=%fused_computation.42 | convolution fusion | flops 13631488 | bytes 4325504 | tf_op jit(solution)/shard_map/dot_general | solution.py:158
  137.1 6.6 %all-gather = f32[128,128]{1,0:T(8,128)S(1)} all-gather(f32[32,128]{1,0:T(8,128)S(1)} %fusion.59), channel_id=2, replica_groups=mesh['groups'=2,'tile'=4,'tracer'=4] {'tracer'}, dimensions={0}, use_global_device_ids=true | all-gather | bytes 81920 | tf_op jit(solution)/shard_map/all_gather | solution.py:39
  143.7 0.3 while.10
  144.0 0.0 copy-done.5
  144.0 0.0 copy-start.4
  144.0 0.0 copy-start.1
  144.0 0.0 copy-start.6
  144.0 4.1 %fusion.64 = f32[32,8,32,128]{3,0,2,1:T(8,128)S(1)} fusion(f32[32,8,32,128]{3,0,2,1:T(8,128)} %fusion.14, s32[32]{0:T(128)S(1)} %copy-done.5), kind=kOutput, calls=%fused_computation.116 | convolution fusion | flops 402654208 | bytes 8388736 | tf_op jit(solution)/shard_map/dot_general | solution.py:176
  148.1 0.0 copy-done.4
  148.1 0.1 fusion.29
  148.2 0.0 collective-permute-done.9
  148.2 0.8 fusion.37
  149.0 4.2 %multiply_add_fusion = f32[32,8,32,128]{3,0,2,1:T(8,128)S(1)} fusion(f32[32,8,32,128]{3,0,2,1:T(8,128)S(1)} %copy-done.1, f32[32,8,32,128]{3,0,2,1:T(8,128)S(1)} %fusion.64, f32[8,32,128]{2,1,0:T(8,128)S(1)} %get-tuple-element.69, f32[32]{0:T(128)S(1)} %copy-done.6, f32[8,32,128]{2,1,0:T(8,128)S(1)} %get-tuple-element.60, s32[32]{0:T(128)S(1)} %copy-done.5), kind=kOutput, calls=%fused_computation.40 | convolution fusion | flops 412091392 | bytes 12845312 | tf_op jit(solution)/shard_map/dot_general | solution.py:184
  153.2 4.4 %copy.17 = f32[32,8,32,128]{3,2,1,0:T(8,128)} copy(f32[32,8,32,128]{3,0,2,1:T(8,128)S(1)} %multiply_add_fusion) | data formatting | bytes 8388608
  (19 shorter events, 0.3 us)
Async XLA Ops:
  0.6 131.9 %copy-start = (f32[32]{0:T(128)S(1)}, f32[32]{0:T(128)}, u32[]{:S(2)}) copy-start(f32[32]{0:T(128)} %param.15) | copy-start | bytes 388
  1.6 22.6 %collective-permute-start = (f32[2,8,2,128]{3,2,1,0:T(2,128)S(1)}, f32[2,8,2,128]{3,2,1,0:T(2,128)S(1)}, u32[]{:S(2)}, u32[]{:S(2)}) collective-permute-start(f32[2,8,2,128]{3,2,1,0:T(2,128)S(1)} %get-tuple-element.53), channel_id=1, source_target_pairs={{0,4},{4,8},{8,12},{12,0},{1,5},{5,9},{9,13},{13,1},{2,6},{6,10},{... | collective-permute-start | bytes 49160 | tf_op jit(solution)/shard_map/ppermute | solution.py:29
  3.7 20.5 %collective-permute-start.1 = (f32[2,8,2,128]{3,2,1,0:T(2,128)S(1)}, f32[2,8,2,128]{3,2,1,0:T(2,128)S(1)}, u32[]{:S(2)}, u32[]{:S(2)}) collective-permute-start(f32[2,8,2,128]{3,2,1,0:T(2,128)S(1)} %get-tuple-element.54), channel_id=1, source_target_pairs={{4,0},{8,4},{12,8},{0,12},{5,1},{9,5},{13,9},{1,13},{6,2},{10,6},{... | collective-permute-start | bytes 49160 | tf_op jit(solution)/shard_map/ppermute | solution.py:32
  6.5 15.8 %collective-permute-start.2 = (s32[2,128]{1,0:T(2,128)S(1)}, s32[2,128]{1,0:T(2,128)S(1)}, u32[]{:S(2)}, u32[]{:S(2)}) collective-permute-start(s32[2,128]{1,0:T(2,128)S(1)} %get-tuple-element.76), channel_id=1, source_target_pairs={{0,4},{4,8},{8,12},{12,0},{1,5},{5,9},{9,13},{13,1},{2,6},{6,10},{... | collective-permute-start | bytes 3080 | tf_op jit(solution)/shard_map/ppermute | solution.py:29
  6.5 17.3 %collective-permute-start.3 = (s32[2,128]{1,0:T(2,128)S(1)}, s32[2,128]{1,0:T(2,128)S(1)}, u32[]{:S(2)}, u32[]{:S(2)}) collective-permute-start(s32[2,128]{1,0:T(2,128)S(1)} %get-tuple-element.77), channel_id=1, source_target_pairs={{4,0},{8,4},{12,8},{0,12},{5,1},{9,5},{13,9},{1,13},{6,2},{10,6},{... | collective-permute-start | bytes 3080 | tf_op jit(solution)/shard_map/ppermute | solution.py:32
  14.6 6.5 %copy-start.2 = (f32[8,32,128]{2,1,0:T(8,128)S(1)}, f32[8,32,128]{2,1,0:T(8,128)}, u32[]{:S(2)}) copy-start(f32[8,32,128]{2,1,0:T(8,128)} %param.12) | copy-start | bytes 393220
  14.6 9.2 %copy-start.3 = (s32[32,128]{1,0:T(8,128)S(1)}, s32[32,128]{1,0:T(8,128)}, u32[]{:S(2)}) copy-start(s32[32,128]{1,0:T(8,128)} %param.13) | copy-start | bytes 49156
  14.6 53.7 %all-to-all-start = ((f32[8,32,32,128]{3,2,0,1:T(8,128)}), f32[8,32,32,128]{3,2,0,1:T(8,128)}, u32[]{:S(2)}, u32[]{:S(2)}) async-start(f32[8,32,32,128]{3,2,0,1:T(8,128)} %copy.14), calls=%async_computation | async-start | bytes 8388608 | tf_op jit(solution)/shard_map/all_to_all | solution.py:108
  21.1 3.5 %collective-permute-start.8 = (f32[8,1,128]{2,1,0:T(1,128)S(1)}, f32[8,1,128]{2,1,0:T(1,128)S(1)}, u32[]{:S(2)}, u32[]{:S(2)}) collective-permute-start(f32[8,1,128]{2,1,0:T(1,128)S(1)} %get-tuple-element.73), channel_id=1, source_target_pairs={{4,0},{8,4},{12,8},{0,12},{5,1},{9,5},{13,9},{1,13},{6,2},{10,6},{... | collective-permute-start | bytes 12296 | tf_op jit(solution)/shard_map/ppermute | solution.py:32
  22.3 125.9 %collective-permute-start.9 = (f32[8,1,128]{2,1,0:T(1,128)S(1)}, f32[8,1,128]{2,1,0:T(1,128)S(1)}, u32[]{:S(2)}, u32[]{:S(2)}) collective-permute-start(f32[8,1,128]{2,1,0:T(1,128)S(1)} %get-tuple-element.72), channel_id=1, source_target_pairs={{0,4},{4,8},{8,12},{12,0},{1,5},{5,9},{9,13},{13,1},{2,6},{6,10},{... | collective-permute-start | bytes 12296 | tf_op jit(solution)/shard_map/ppermute | solution.py:29
  75.8 12.1 %collective-permute-start.4 = (f32[32,8,2,128]{3,0,2,1:T(8,128)S(1)}, f32[32,8,2,128]{3,0,2,1:T(8,128)S(1)}, u32[]{:S(2)}, u32[]{:S(2)}) collective-permute-start(f32[32,8,2,128]{3,0,2,1:T(8,128)S(1)} %get-tuple-element.51), channel_id=1, source_target_pairs={{0,4},{4,8},{8,12},{12,0},{1,5},{5,9},{9,13},{13,1},{2,6},{6,10},{... | collective-permute-start | bytes 786440 | tf_op jit(solution)/shard_map/ppermute | solution.py:29
  75.8 12.7 %collective-permute-start.5 = (f32[32,8,2,128]{3,0,2,1:T(8,128)S(1)}, f32[32,8,2,128]{3,0,2,1:T(8,128)S(1)}, u32[]{:S(2)}, u32[]{:S(2)}) collective-permute-start(f32[32,8,2,128]{3,0,2,1:T(8,128)S(1)} %get-tuple-element.52), channel_id=1, source_target_pairs={{4,0},{8,4},{12,8},{0,12},{5,1},{9,5},{13,9},{1,13},{6,2},{10,6},{... | collective-permute-start | bytes 786440 | tf_op jit(solution)/shard_map/ppermute | solution.py:32
  102.4 10.8 %collective-permute-start.6 = (f32[32,8,2,128]{3,0,2,1:T(8,128)S(1)}, f32[32,8,2,128]{3,0,2,1:T(8,128)S(1)}, u32[]{:S(2)}, u32[]{:S(2)}) collective-permute-start(f32[32,8,2,128]{3,0,2,1:T(8,128)S(1)} %get-tuple-element.47), channel_id=1, source_target_pairs={{0,4},{4,8},{8,12},{12,0},{1,5},{5,9},{9,13},{13,1},{2,6},{6,10},{... | collective-permute-start | bytes 786440 | tf_op jit(solution)/shard_map/ppermute | solution.py:29
  102.5 13.5 %collective-permute-start.7 = (f32[32,8,2,128]{3,0,2,1:T(8,128)S(1)}, f32[32,8,2,128]{3,0,2,1:T(8,128)S(1)}, u32[]{:S(2)}, u32[]{:S(2)}) collective-permute-start(f32[32,8,2,128]{3,0,2,1:T(8,128)S(1)} %get-tuple-element.48), channel_id=1, source_target_pairs={{4,0},{8,4},{12,8},{0,12},{5,1},{9,5},{13,9},{1,13},{6,2},{10,6},{... | collective-permute-start | bytes 786440 | tf_op jit(solution)/shard_map/ppermute | solution.py:32
  132.5 11.5 %copy-start.5 = (s32[32]{0:T(128)S(1)}, s32[32]{0:T(128)}, u32[]{:S(2)}) copy-start(s32[32]{0:T(128)} %param.14) | copy-start | bytes 388
  144.0 4.1 %copy-start.4 = (f32[32,128]{1,0:T(8,128)S(1)}, f32[32,128]{1,0:T(8,128)}, u32[]{:S(2)}) copy-start(f32[32,128]{1,0:T(8,128)} %param.17) | copy-start | bytes 49156
  144.0 5.0 %copy-start.1 = (f32[32,8,32,128]{3,0,2,1:T(8,128)S(1)}, f32[32,8,32,128]{3,0,2,1:T(8,128)}, u32[]{:S(2)}) copy-start(f32[32,8,32,128]{3,0,2,1:T(8,128)} %fusion.14) | copy-start | bytes 12582916
  144.0 5.0 %copy-start.6 = (f32[32]{0:T(128)S(1)}, f32[32]{0:T(128)}, u32[]{:S(2)}) copy-start(f32[32]{0:T(128)} %param.16) | copy-start | bytes 388
where the time goes:
time: 158 us
  other arithmetic  46.2 us (29%)
  waiting for transfers between devices  46.1 us (29%)
  local copies, waits for them, and re-layouts  22.5 us (14%)
  starting transfers between devices  22.2 us (14%)
  matrix products  12.8 us (8%)
  blocking collectives  6.62 us (4%)
    all_to_all x1, waiting for transfers between devices, to_cells(): lax.all_to_all(values, 'tracer', split_axis=1, concat_axis=0, tiled=True)  42.6 us
    select_n x4, other arithmetic, face_flux(): return jnp.where(speed > 0.0, positive, negative)  28.3 us
    sub x2, other arithmetic, flux_substep(): return middle - sub_step * spread  15.5 us
    ppermute x5, starting transfers between devices, padded(): lax.ppermute(lax.slice_in_dim(block, 0, width, axis=dim), axis, backward)  11.9 us
    unnamed x16, local copies, waits for them, and re-layouts  9.32 us
    all_gather x1, blocking collectives, prefix(): gathered = lax.all_gather(part, axis)  6.62 us
    all_to_all x1, starting transfers between devices, to_cells(): lax.all_to_all(values, 'tracer', split_axis=1, concat_axis=0, tiled=True)  6.46 us
    all_to_all x1, local copies, waits for them, and re-layouts, to_cells(): lax.all_to_all(values, 'tracer', split_axis=1, concat_axis=0, tiled=True)  4.56 us
  transfers between devices with their start and end apart: 11, of which 3 were waited for; matrix products, arithmetic and copies ran while one was open for 45% of the time, Pallas kernels for 0%

commit v1 on v0

v1 whole, which is shorter than its diff:
```python
import functools

import jax
import jax.numpy as jnp
from jax import lax
from jax.experimental import pallas as pl
from jax.experimental.pallas import tpu as pltpu
from jax.sharding import PartitionSpec as P

sub_step = 0.45
step_duration = 0.2
gravity = 0.5
viscosity = 0.2
coriolis_base = 0.5
beta_plane = 0.5
spreading_coefficient = 0.2
water_clear = 0.05
column_optical = 3.0
warming_coefficient = 5.0
light_half = 0.3
nutrient_half = 0.5

SUB = 8
REACH = 4
EXTRA = 8


def shift_south(values):
    return jnp.concatenate([jnp.zeros_like(values[..., :1]), values[..., :-1]], axis=-1)


def shift_north(values, offset=1):
    return jnp.concatenate([values[..., offset:], jnp.zeros_like(values[..., :offset])], axis=-1)


def laplacian(values):
    inner = values[:, 1:-1]
    return values[:, 2:] + values[:, :-2] + shift_north(inner) + shift_south(inner) - 4.0 * inner


def velocity_advance(flow_one, marine_mask_profile, thermal_profile_alone):
    east_vel = flow_one[0]
    north_vel = flow_one[1]
    ocean_profiles = east_vel.shape[1] - 2
    coriolis_y = (
        coriolis_base
        + beta_plane * jnp.arange(east_vel.shape[2], dtype=jnp.float32) / east_vel.shape[2]
    )
    centre_u = east_vel[:, 1 : ocean_profiles + 1]
    centre_v = north_vel[:, 1 : ocean_profiles + 1]
    v_bar = 0.25 * (
        centre_v + north_vel[:, 2:] + shift_south(centre_v) + shift_south(north_vel[:, 2:])
    )
    u_bar = 0.25 * (
        centre_u + east_vel[:, :-2] + shift_north(centre_u) + shift_north(east_vel[:, :-2])
    )
    marine_mask_interior = marine_mask_profile[:, 1 : ocean_profiles + 1]
    east_open = marine_mask_interior * marine_mask_profile[:, 2:]
    north_open = marine_mask_interior * shift_north(marine_mask_interior)
    heat_mid = thermal_profile_alone[:, 1 : ocean_profiles + 1]
    new_east = east_open * (
        centre_u
        + step_duration
        * (
            coriolis_y * v_bar
            - gravity * (thermal_profile_alone[:, 2:] - heat_mid)
            + viscosity * laplacian(east_vel)
        )
    )
    new_north = north_open * (
        centre_v
        + step_duration
        * (
            -coriolis_y * u_bar
            - gravity * (shift_north(heat_mid) - heat_mid)
            + viscosity * laplacian(north_vel)
        )
    )
    return jnp.stack([new_east, new_north]), laplacian(thermal_profile_alone)


def pack_kernel(
    tracers, own_levels, c_low, c_high, uv_low, uv_high, heat, depth, to_next, to_previous
):
    rows = depth.shape[0]
    base = REACH * tracers
    for t in range(tracers):
        place = pl.ds(REACH * t, REACH)
        to_next[:, place, :] = c_high[t, :, SUB - REACH :, :]
        to_previous[:, place, :] = c_low[t, :, :REACH, :]
    to_next[:, base : base + 3, :] = uv_high[0, :, SUB - 3 :, :]
    to_next[:, base + 3 : base + 5, :] = uv_high[1, :, SUB - 2 :, :]
    to_previous[:, base : base + 3, :] = uv_low[0, :, :3, :]
    to_previous[:, base + 3 : base + 5, :] = uv_low[1, :, :2, :]

    @pl.when(pl.program_id(0) == 0)
    def _():
        for level in range(own_levels):
            to_next[level, base + 5 : base + 6, :] = heat[level, rows - 1 : rows, :]
            to_previous[level, base + 5 : base + 6, :] = heat[level, 0:1, :]
        for row in range(REACH):
            start = rows - REACH + row
            to_next[row, base + 6 : base + 7, :] = depth[start : start + 1, :].astype(jnp.float32)
            to_previous[row, base + 6 : base + 7, :] = depth[row : row + 1, :].astype(jnp.float32)


def pack(species, currents, heat, depth):
    tracers, levels, rows, width = species.shape
    height = REACH * tracers + EXTRA
    last = rows // SUB - 1
    out = jax.ShapeDtypeStruct((levels, height, width), jnp.float32)
    out_spec = pl.BlockSpec((SUB, height, width), lambda g: (g, 0, 0))
    return pl.pallas_call(
        functools.partial(pack_kernel, tracers, heat.shape[0]),
        grid=(levels // SUB,),
        in_specs=[
            pl.BlockSpec((tracers, SUB, SUB, width), lambda g: (0, g, 0, 0)),
            pl.BlockSpec((tracers, SUB, SUB, width), lambda g: (0, g, last, 0)),
            pl.BlockSpec((2, SUB, SUB, width), lambda g: (0, g, 0, 0)),
            pl.BlockSpec((2, SUB, SUB, width), lambda g: (0, g, last, 0)),
            pl.BlockSpec(heat.shape, lambda g: (0, 0, 0)),
            pl.BlockSpec(depth.shape, lambda g: (0, 0)),
        ],
        out_specs=[out_spec, out_spec],
        out_shape=[out, out],
        name="pack",
        cost_estimate=pl.CostEstimate(
            flops=0, transcendentals=0, bytes_accessed=levels * height * width * 4 * 4
        ),
    )(species, species, currents, currents, heat, depth)


class Rows:
    def __init__(self, cells, east, north, lanes):
        self.cells, self.east, self.north = cells, east, north
        self.first, self.last = lanes
        self.kept = {}

    def keep(self, name, row, make):
        key = (name, row)
        if key not in self.kept:
            self.kept[key] = make()
        return self.kept[key]

    def half(self, row):
        return self.keep("half", row, lambda: 0.5 * self.cells(row))

    def slope(self, row):
        return self.keep("slope", row, lambda: self.half(row + 1) - self.half(row))

    def edges(self, row):
        def make():
            limited = limit(self.slope(row - 1), self.slope(row))
            return self.cells(row) + limited, self.cells(row) - limited

        return self.keep("edges", row, make)

    def east_flux(self, row):
        def make():
            speed = self.east(row)
            return speed * jnp.where(speed > 0.0, self.edges(row)[0], self.edges(row + 1)[1])

        return self.keep("flux", row, make)

    def north_spread(self, row):
        width = self.half(row).shape[1]
        half = self.half(row)
        slope = jnp.where(self.last, 0.0, pltpu.roll(half, width - 1, 1)) - half
        before = jnp.where(self.first, half, pltpu.roll(slope, 1, 1))
        limited = limit(before, slope)
        speed = self.north(row)
        cell = self.cells(row)
        ahead = pltpu.roll(cell - limited, width - 1, 1)
        flux = speed * jnp.where(speed > 0.0, cell + limited, ahead)
        return flux - pltpu.roll(flux, 1, 1)

    def new(self, row):
        def make():
            spread = (self.east_flux(row) - self.east_flux(row - 1)) + self.north_spread(row)
            return self.cells(row) - spread

        return self.keep("new", row, make)


def limit(one, other):
    low = jnp.minimum(one, other)
    high = jnp.maximum(one, other)
    return jnp.maximum(low, jnp.minimum(high, 0.0))


def advect_kernel(
    plan, me_ref, attenuation, c_ref, uv_ref, depth_ref, *refs
):
    rows, levels, tracers_here, first, count, own, low, high, width = (
        plan["rows"],
        plan["levels"],
        plan["tracers"],
        plan["first"],
        plan["count"],
        plan["own_levels"],
        plan["low"],
        plan["high"],
        plan["width"],
    )
    devices = levels // own
    shared, pieces = max(1, SUB // own), max(1, own // SUB)
    tall = high - low
    main = own * count * tall
    if plan["halo"]:
        halo_ref, halo_top = refs[:2]
        refs = refs[2:]
    outs = refs[:devices]
    buffer, east, north, shade, sums, sems = refs[devices:]
    height = REACH * tracers_here + EXTRA
    base = REACH * tracers_here
    me = me_ref[0]
    step = pl.program_id(0)
    if shared > 1:
        group = lax.bitwise_xor(me // shared, step)
    else:
        group = lax.bitwise_xor(me, step // pieces) * pieces + lax.rem(step, pieces)

    lane = lax.broadcasted_iota(jnp.int32, (SUB, width), 1)
    lanes = (lane == 0, lane == width - 1)
    level = group * SUB + lax.broadcasted_iota(jnp.int32, (SUB, width), 0)

    def halo_row(row):
        return REACH + row if row < 0 else row - rows

    def depth_row(row):
        if 0 <= row < rows:
            line = depth_ref[row : row + 1, :]
        else:
            at = halo_row(row) * height + base + 6
            line = halo_top[at : at + 1, :].astype(jnp.int32)
        return jnp.broadcast_to(line, (SUB, width))

    def speed_row(which, row):
        if 0 <= row < rows:
            return uv_ref[which, pl.ds(row, SUB, stride=rows), :]
        if row < 0:
            at = base + (3 + row if which == 0 else 5 + row)
        else:
            at = base + 3 * which + row - rows
        return halo_ref[pl.ds(at, SUB, stride=height), :]

    here = depth_row(low - 3)
    for row in range(low - 3, high + 2):
        above = depth_row(row + 1)
        at = row - (low - 3)
        open_east = level < jnp.minimum(here, above)
        east[at] = jnp.where(open_east, sub_step * speed_row(0, row), 0.0)
        if row >= low - 2:
            beyond = jnp.where(lanes[1], 0, pltpu.roll(here, width - 1, 1))
            open_north = level < jnp.minimum(here, beyond)
            north[at] = jnp.where(open_north, sub_step * speed_row(1, row), 0.0)
        here = above

    for row in range(tall):
        shade[row] = jnp.zeros((SUB, width), jnp.float32)

    def one(t):
        def cell(row):
            if 0 <= row < rows:
                return c_ref[t + plan["skip"], pl.ds(row, SUB, stride=rows), :]
            at = REACH * (t + first) + halo_row(row)
            return halo_ref[pl.ds(at, SUB, stride=height), :]

        kept = {}

        def cells(row):
            if row not in kept:
                kept[row] = cell(row)
            return kept[row]

        def east_speed(row):
            return east[row - (low - 3)]

        def north_speed(row):
            return north[row - (low - 3)]

        before = Rows(cells, east_speed, north_speed, lanes)
        return Rows(before.new, east_speed, north_speed, lanes)

    unroll = plan["unroll"]

    def some(index, _):
        numbers = [index * unroll + k for k in range(unroll)]
        streams = [one(t) for t in numbers]
        factors = [attenuation[me * tracers_here + first + t] for t in numbers]
        for row in range(low, high):
            total = shade[row - low]
            for t, stream, factor in zip(numbers, streams, factors):
                value = stream.new(row)
                total = total + factor * jnp.abs(value)
                start = t * tall + row - low
                if shared > 1:
                    for part in range(shared):
                        slot = lax.bitwise_xor(me, group * shared + part)
                        buffer[slot, pl.ds(start, own, stride=count * tall), :] = value[
                            part * own : (part + 1) * own
                        ]
                else:
                    start = start + lax.rem(step, pieces) * SUB * count * tall
                    buffer[step // pieces, pl.ds(start, SUB, stride=count * tall), :] = value
            shade[row - low] = total
        return 0

    lax.fori_loop(0, count // unroll, some, 0)

    for part in range(shared):
        dest = group * shared + part if shared > 1 else group // pieces
        for row in range(tall):
            value = shade[row][part * min(own, SUB) : (part + 1) * min(own, SUB)]
            line = jnp.sum(value, axis=0, keepdims=True)
            if pieces > 1:
                old = jnp.where(lax.rem(step, pieces) == 0, 0.0, sums[dest, row : row + 1, :])
                line = line + old
            sums[dest, row : row + 1, :] = line

    def copy(slot, start, size, which):
        at = pl.ds(start, size)
        return pltpu.make_async_copy(
            buffer.at[slot, at, :], outs[slot].at[at, :], sems.at[slot, which]
        )

    for slot in range(devices):

        @pl.when(step == (slot // shared) * pieces + pieces - 1)
        def _():
            copy(slot, 0, main, 0).start()

    @pl.when(step == levels // SUB - 1)
    def _():
        for slot in range(devices):
            dest = lax.bitwise_xor(me, slot)
            above = jnp.zeros((tall, width), jnp.float32)
            for other in range(devices):
                above = above + jnp.where(other < dest, sums[other], 0.0)
            buffer[slot, main : main + tall, :] = above
        for slot in range(devices):
            copy(slot, main, tall, 1).start()
        for slot in range(devices):
            copy(slot, 0, main, 0).wait()
            copy(slot, main, tall, 1).wait()


def advect(species, currents, depth, attenuation, me, devices, first, count, low, high, halo, name):
    tracers, levels, rows, width = species.shape
    own = levels // devices
    shared, pieces = max(1, SUB // own), max(1, own // SUB)
    tall = high - low
    total = (own * count + 1) * tall
    height = REACH * tracers + EXTRA
    block = count if first % count == 0 else tracers
    plan = dict(
        rows=rows,
        levels=levels,
        tracers=tracers,
        first=first,
        count=count,
        own_levels=own,
        low=low,
        high=high,
        width=width,
        halo=halo is not None,
        skip=0 if block == count else first,
        unroll=2 if count % 2 == 0 else 1,
    )

    def group(step, me_ref):
        if shared > 1:
            return lax.bitwise_xor(me_ref[0] // shared, step)
        return lax.bitwise_xor(me_ref[0], step // pieces) * pieces + lax.rem(step, pieces)

    in_specs = [
        pl.BlockSpec(memory_space=pltpu.SMEM),
        pl.BlockSpec(
            (block, SUB * rows, width),
            lambda q, m: (first // count if block == count else 0, group(q, m), 0),
        ),
        pl.BlockSpec((2, SUB * rows, width), lambda q, m: (0, group(q, m), 0)),
        pl.BlockSpec((rows, width), lambda q, m: (0, 0)),
    ]
    args = [
        me,
        attenuation,
        species.reshape(tracers, levels * rows, width),
        currents.reshape(2, levels * rows, width),
        depth,
    ]
    if halo is not None:
        flat = halo.reshape(levels * height, width)
        in_specs += [
            pl.BlockSpec((SUB * height, width), lambda q, m: (group(q, m), 0)),
            pl.BlockSpec((SUB * height, width), lambda q, m: (0, 0)),
        ]
        args += [flat, flat]
    area = tall * width * levels * count
    return pl.pallas_call(
        functools.partial(advect_kernel, plan),
        grid_spec=pltpu.PrefetchScalarGridSpec(
            num_scalar_prefetch=1,
            grid=(levels // SUB,),
            in_specs=in_specs,
            out_specs=[pl.BlockSpec(memory_space=pl.ANY)] * devices,
            scratch_shapes=[
                pltpu.VMEM((devices, total, width), jnp.float32),
                pltpu.VMEM((tall + 5, SUB, width), jnp.float32),
                pltpu.VMEM((tall + 5, SUB, width), jnp.float32),
                pltpu.VMEM((tall, SUB, width), jnp.float32),
                pltpu.VMEM((devices, tall, width), jnp.float32),
                pltpu.SemaphoreType.DMA((devices, 2)),
            ],
        ),
        out_shape=[jax.ShapeDtypeStruct((total, width), jnp.float32)] * devices,
        name=name,
        cost_estimate=pl.CostEstimate(
            flops=area * 60, transcendentals=0, bytes_accessed=area * 16
        ),
    )(*args)


def react_kernel(plan, me_ref, consumed, attenuation, speeds, *refs):
    counts, tracers_here, own, devices, block, tall, width, levels = (
        plan["counts"],
        plan["tracers"],
        plan["own_levels"],
        plan["devices"],
        plan["block"],
        plan["tall"],
        plan["width"],
        plan["levels"],
    )
    parts = len(counts)
    data = [refs[p * devices : (p + 1) * devices] for p in range(parts)]
    refs = refs[parts * devices :]
    planes = refs[: parts * devices]
    refs = refs[parts * devices :]
    sun, depth, heat = refs[:3]
    out, heat_out, above, gain, share, inverse = refs[3 + plan["aliased"] :]
    me = me_ref[0]
    first_level = me * own + pl.program_id(0) * block
    band = pl.program_id(1)
    at = pl.ds(pl.multiple_of(band * SUB, SUB), SUB)
    layer = column_optical / levels

    @pl.when((pl.program_id(0) == 0) & (band == 0))
    def _():
        total = planes[0][...]
        for plane in planes[1:]:
            total = total + plane[...]
        above[...] = (total + (me * own).astype(jnp.float32) * water_clear) * layer

        def fill(t, _):
            inverse[consumed[t]] = t
            return 0

        lax.fori_loop(0, devices * tracers_here, fill, 0)

    pieces = []
    first = 0
    for p, count in enumerate(counts):
        pieces += [(p, slot, t, first + t) for slot in range(devices) for t in range(count)]
        first += count

    def one(level, _):
        def load(p, slot, t):
            offset = (level * counts[p] + t) * tall + band * SUB
            return data[p][slot][pl.ds(pl.multiple_of(offset, SUB), SUB), :]

        total = jnp.zeros((SUB, width), jnp.float32)
        for p, slot, t, local in pieces:
            number = lax.bitwise_xor(me, slot) * tracers_here + local
            value = load(p, slot, t)
            size = jnp.abs(value)
            total = total + attenuation[number] * size
            share[number] = value / (nutrient_half + size)
            gain[number] = speeds[number] * value
        optical = (water_clear + total) * layer
        overhead = above[at, :]
        above[at, :] = overhead + optical
        caught = sun[...] * jnp.exp(-overhead) * (1.0 - jnp.exp(-optical))
        mean_light = caught / optical
        wet = jnp.where(first_level + level < depth[...], 1.0, 0.0)
        light = wet * (mean_light / (mean_light + light_half))
        heat_out[level] = wet * (heat[level] + warming_coefficient * (caught * wet))
        for p, slot, t, local in pieces:
            number = lax.bitwise_xor(me, slot) * tracers_here + local
            taken = gain[number] * share[consumed[number]]
            lost = gain[inverse[number]] * share[number]
            out[number, level] = load(p, slot, t) + light * (taken - lost)
        return 0

    lax.fori_loop(0, block, one, 0)


def react(parts, counts, me, consumed, attenuation, speeds, sun, depth, heat, old, low, high, block, levels, name):
    devices = len(parts[0])
    rows, width = sun.shape
    own = heat.shape[0]
    tracers_here = sum(counts)
    every = devices * tracers_here
    tall = high - low
    place = low // SUB
    plan = dict(
        counts=counts,
        tracers=tracers_here,
        own_levels=own,
        devices=devices,
        block=block,
        tall=tall,
        width=width,
        levels=levels,
        aliased=0 if old is None else 2,
    )
    smem = pl.BlockSpec(memory_space=pltpu.SMEM)
    in_specs = [smem, smem, smem]
    args = [me, consumed, attenuation, speeds]
    for part, count in zip(parts, counts):
        in_specs += [pl.BlockSpec((block * count * tall, width), lambda q, r, m: (q, 0))] * devices
        args += part
    for part, count in zip(parts, counts):
        in_specs += [pl.BlockSpec((tall, width), lambda q, r, m, at=own * count: (at, 0))] * devices
        args += part
    band = pl.BlockSpec((SUB, width), lambda q, r, m: (place + r, 0))
    heat_spec = pl.BlockSpec((block, SUB, width), lambda q, r, m: (q, place + r, 0))
    in_specs += [band, band, heat_spec]
    args += [sun, depth, heat]
    aliases = {}
    if old is not None:
        aliases = {len(args): 0, len(args) + 1: 1}
        in_specs += [pl.BlockSpec(memory_space=pl.ANY)] * 2
        args += list(old)
    area = tall * width * own * every
    return pl.pallas_call(
        functools.partial(react_kernel, plan),
        grid_spec=pltpu.PrefetchScalarGridSpec(
            num_scalar_prefetch=1,
            grid=(own // block, tall // SUB),
            in_specs=in_specs,
            out_specs=[
                pl.BlockSpec((every, block, SUB, width), lambda q, r, m: (0, q, place + r, 0)),
                heat_spec,
            ],
            scratch_shapes=[
                pltpu.VMEM((tall, width), jnp.float32),
                pltpu.VMEM((every, SUB, width), jnp.float32),
                pltpu.VMEM((every, SUB, width), jnp.float32),
                pltpu.SMEM((every,), jnp.int32),
            ],
        ),
        out_shape=[
            jax.ShapeDtypeStruct((every, own, rows, width), jnp.float32),
            jax.ShapeDtypeStruct(heat.shape, jnp.float32),
        ],
        input_output_aliases=aliases,
        name=name,
        cost_estimate=pl.CostEstimate(flops=area * 20, transcendentals=0, bytes_accessed=area * 8),
    )(*args)


def exchange(blocks, axis):
    devices = len(blocks)
    got = {0: blocks[0]}
    for offset in sorted(range(1, devices), reverse=True):
        pairs = [(i, i ^ offset) for i in range(devices)]
        got[offset] = lax.ppermute(blocks[offset], axis, pairs)
    return [got[k] for k in range(devices)]


def on_device(
    species,
    currents,
    heat,
    depth,
    consumed,
    attenuation,
    speeds,
    sun,
):
    devices = lax.axis_size("tracer")
    tiles = lax.axis_size("tile")
    tracers, levels, rows, width = species.shape
    own = heat.shape[0]
    place = lax.axis_index("tracer")
    me = place.astype(jnp.int32).reshape(1)
    forward = [(i, (i + 1) % tiles) for i in range(tiles)]
    backward = [(target, source) for source, target in forward]
    edge = SUB
    half = tracers // 2
    base = REACH * tracers

    send = functools.partial(advect, species, currents, depth, attenuation, me, devices)
    inner_a = exchange(send(0, half, edge, rows - edge, None, "inner_a"), "tracer")
    to_next, to_previous = pack(species, currents, heat, depth)
    from_previous = lax.ppermute(to_next, "tile", forward)
    from_next = lax.ppermute(to_previous, "tile", backward)
    inner_b = exchange(send(half, tracers - half, edge, rows - edge, None, "inner_b"), "tracer")
    top = exchange(send(0, tracers, 0, edge, from_previous, "top"), "tracer")
    bottom = exchange(send(0, tracers, rows - edge, rows, from_next, "bottom"), "tracer")

    first_level = place * own
    below = lax.dynamic_slice_in_dim(from_previous, first_level, own, 0)
    above = lax.dynamic_slice_in_dim(from_next, first_level, own, 0)
    flow = lax.dynamic_slice_in_dim(currents, first_level, own, 1)
    flow_one = jnp.stack(
        [
            jnp.concatenate(
                [below[:, base + 2 : base + 3], flow[0], above[:, base : base + 1]], axis=1
            ),
            jnp.concatenate(
                [below[:, base + 4 : base + 5], flow[1], above[:, base + 3 : base + 4]], axis=1
            ),
        ]
    )
    heat_one = jnp.concatenate(
        [
            from_previous[:own, base + 5 : base + 6],
            heat,
            from_next[:own, base + 5 : base + 6],
        ],
        axis=1,
    )
    depth_one = jnp.concatenate(
        [
            from_previous[REACH - 1 : REACH, base + 6].astype(jnp.int32),
            depth,
            from_next[0:1, base + 6].astype(jnp.int32),
        ],
        axis=0,
    )
    level_numbers = first_level + jnp.arange(own, dtype=jnp.int32)
    wet_one = (level_numbers[:, None, None] < depth_one[None]).astype(jnp.float32)
    velocity, heat_curve = velocity_advance(flow_one, wet_one, heat_one)
    calm = heat + step_duration * spreading_coefficient * heat_curve

    def finish(parts, counts, old, low, high, block, name):
        return react(
            parts,
            counts,
            me,
            consumed,
            attenuation,
            speeds,
            sun,
            depth,
            calm,
            old,
            low,
            high,
            block,
            levels,
            name,
        )

    block = max(1, own // 2)
    done = finish(
        [inner_a, inner_b], [half, tracers - half], None, edge, rows - edge, block, "react_inner"
    )
    done = finish([top], [tracers], done, 0, edge, block, "react_top")
    done = finish([bottom], [tracers], done, rows - edge, rows, block, "react_bottom")
    return done[0], velocity, done[1]


def solution(mesh):
    return jax.shard_map(
        on_device,
        mesh=mesh,
        in_specs=(
            P(("groups", "tracer"), None, "tile", None),
            P(None, "groups", "tile", None),
            P(("groups", "tracer"), "tile", None),
            P(("groups", "tile"), None),
            P(),
            P(),
            P(),
            P(("groups", "tile"), None),
        ),
        out_specs=(
            P("groups", "tracer", "tile", None),
            P(None, ("groups", "tracer"), "tile", None),
            P(("groups", "tracer"), "tile", None),
        ),
        check_vma=False,
    )
```

time: 158 us -> 97.4 us (0.62)
  Pallas kernels: 0 us -> 59.5 us
  other arithmetic: 46.2 us -> 2.94 us
  waiting for transfers between devices: 46.1 us -> 14.1 us
  local copies, waits for them, and re-layouts: 22.5 us -> 3.4 us
  matrix products: 12.8 us -> 0 us
  blocking collectives: 6.62 us -> 0 us
  starting transfers between devices: 22.2 us -> 16.1 us
    pallas_call x0 -> x8, Pallas kernels: none -> 59.5 us  [the longest x4 42.6 us: advect(): pl.pallas_call(functools.partial(advect_kernel, plan), grid_spec=pltpu.Pr...]
    all_to_all x1 -> x0, waiting for transfers between devices: 42.6 us -> none  [to_cells(): lax.all_to_all(values, 'tracer', split_axis=1, concat_axis=0, tiled=True)]
    select_n x4 -> x0, other arithmetic: 28.3 us -> none  [face_flux(): return jnp.where(speed > 0.0, positive, negative)]
    sub x2 -> x0, other arithmetic: 15.5 us -> none  [flux_substep(): return middle - sub_step * spread]
    dot_general x3 -> x0, matrix products: 12.8 us -> none  [the longest x1 4.54 us: optical_thickness(): jnp.tensordot(attenuation_factor, jnp.abs(by_cells), axes=1, precision=la...]
    ppermute x10 -> x14, waiting for transfers between devices: 3.51 us -> 14.1 us  [the longest x12 9.11 us: exchange(): got[offset] = lax.ppermute(blocks[offset], axis, pairs)]
    unnamed x16 -> x28, local copies, waits for them, and re-layouts: 9.32 us -> 1.45 us
    all_gather x1 -> x0, blocking collectives: 6.62 us -> none  [prefix(): gathered = lax.all_gather(part, axis)]
  transfers between devices with their start and end apart: 11 -> 14, of which waited for: 3 -> 4; matrix products, arithmetic and copies ran while one was open for 45% -> 5% of each run, Pallas kernels for 0% -> 54%
where the time goes in v1:
time: 97.4 us; the launch traced here: 96.9 us
  Pallas kernels  59.5 us (61%)
  starting transfers between devices  16.1 us (17%)
  waiting for transfers between devices  14.1 us (14%)
  local copies, waits for them, and re-layouts  3.4 us (3%)
  other arithmetic  2.94 us (3%)
    pallas_call x4, Pallas kernels, advect(): pl.pallas_call(functools.partial(advect_kernel, plan), grid_spec=pltpu.Pr...  42.6 us
    pallas_call x3, Pallas kernels, react(): pl.pallas_call(functools.partial(react_kernel, plan), grid_spec=pltpu.Pre...  13 us
    ppermute x12, starting transfers between devices, exchange(): got[offset] = lax.ppermute(blocks[offset], axis, pairs)  12 us
    ppermute x12, waiting for transfers between devices, exchange(): got[offset] = lax.ppermute(blocks[offset], axis, pairs)  9.11 us
    ppermute x1, waiting for transfers between devices, on_device(): from_previous = lax.ppermute(to_next, 'tile', forward)  5.03 us
    ppermute x1, starting transfers between devices, on_device(): from_next = lax.ppermute(to_previous, 'tile', backward)  4.14 us
    pallas_call x1, Pallas kernels, pack(): pl.pallas_call(functools.partial(pack_kernel, tracers, heat.shape[0]), gr...  3.8 us
    another operation x3, other arithmetic, velocity_advance(): return (jnp.stack([new_east, new_north]), laplacian(thermal_profile_alone))  2.05 us
  transfers between devices with their start and end apart: 14, of which 4 were waited for; matrix products, arithmetic and copies ran while one was open for 5% of the time, Pallas kernels for 54%

profile of v1, /device:TPU:1, one launch (start us, length us, event | category | flops | bytes accessed | tf_op | source)
XLA Modules:
  0.0 96.9 jit_solution(11935512112344635437)
XLA Ops:
  0.6 3.8 %pack.1 = (f32[32,40,128]{2,1,0:T(8,128)}, f32[32,40,128]{2,1,0:T(8,128)}) custom-call(f32[8,32,32,128]{3,2,1,0:T(8,128)} %c_high.1, f32[8,32,32,128]{3,2,1,0:T(8,128)} %c_high.1, f32[2,32,32,128]{3,2,1,0:T(8,128)} %uv_high.1, f32[2,32,32,128]{3,2,1,0:T(8,128)} %uv_high.1, f32[8,32,128]{2,1,0:T(8,128)} %heat.1, s32[32,128]{1,0:T(8,128)} %refs_9_.3), custom_call_target="tpu_custom_call" | custom-call | bytes 2621440 | tf_op jit(solution)/shard_map/pack/pallas_call | solution.py:113
  4.4 4.1 %collective-permute-start = (f32[32,40,128]{2,1,0:T(8,128)}, f32[32,40,128]{2,1,0:T(8,128)S(1)}, u32[]{:S(2)}, u32[]{:S(2)}) collective-permute-start(f32[32,40,128]{2,1,0:T(8,128)} %get-tuple-element.27), channel_id=1, source_target_pairs={{4,0},{8,4},{12,8},{0,12},{5,1},{9,5},{13,9},{1,13},{6,2},{10,6},{... | collective-permute-start | bytes 1966088 | tf_op jit(solution)/shard_map/ppermute | solution.py:598
  8.6 0.0 collective-permute-start.4
  8.6 8.7 %inner_a.1 = (f32[528,128]{1,0:T(8,128)}, f32[528,128]{1,0:T(8,128)}, f32[528,128]{1,0:T(8,128)}, f32[528,128]{1,0:T(8,128)}) custom-call(s32[1]{0:T(128)} %bitcast.me_ref, f32[32]{0:T(128)} %attenuation.13, f32[8,1024,128]{2,1,0:T(8,128)} %bitcast.17, f32[2,1024,128]{2,1,0:T(8,128)} %bitcast.21, s32[32,128]{1,0:T(8,128)} %refs_9_.3), custom_call_target="tpu_custom_call" | custom-call | flops 15728640 | bytes 4194304 | tf_op jit(solution)/shard_map/inner_a/pallas_call | solution.py:400
  17.2 0.0 copy-start
  17.2 0.0 copy-start.3
  17.3 2.1 %collective-permute-start.10 = (f32[528,128]{1,0:T(8,128)}, f32[528,128]{1,0:T(8,128)S(1)}, u32[]{:S(2)}, u32[]{:S(2)}) collective-permute-start(f32[528,128]{1,0:T(8,128)} %get-tuple-element.40), channel_id=1, source_target_pairs={{0,3},{1,2},{2,1},{3,0},{4,7},{5,6},{6,5},{7,4},{8,11},{9,10},{10,... | collective-permute-start | bytes 811016 | tf_op jit(solution)/shard_map/ppermute | solution.py:568
  19.4 8.6 %inner_b.1 = (f32[528,128]{1,0:T(8,128)}, f32[528,128]{1,0:T(8,128)}, f32[528,128]{1,0:T(8,128)}, f32[528,128]{1,0:T(8,128)}) custom-call(s32[1]{0:T(128)} %bitcast.me_ref, f32[32]{0:T(128)} %attenuation.13, f32[8,1024,128]{2,1,0:T(8,128)} %bitcast.18, f32[2,1024,128]{2,1,0:T(8,128)} %bitcast.22, s32[32,128]{1,0:T(8,128)} %refs_9_.3), custom_call_target="tpu_custom_call" | custom-call | flops 15728640 | bytes 4194304 | tf_op jit(solution)/shard_map/inner_b/pallas_call | solution.py:400
  28.0 0.1 collective-permute-start.11
  28.1 0.3 collective-permute-start.12
  28.4 1.0 %dynamic-slice_bitcast_fusion.1 = (f32[8,32,128]{2,1,0:T(8,128)S(1)}, f32[8,32,128]{2,1,0:T(8,128)S(1)}) fusion(f32[2,32,32,128]{3,2,1,0:T(8,128)} %uv_high.1, s32[]{:T(128)S(6)} %select_n.2, s32[]{:T(128)S(6)} %add.131), kind=kLoop, calls=%fused_computation.41 | loop fusion | bytes 524296 | tf_op jit(solution)/shard_map/squeeze | solution.py:610
  29.4 0.0 copy-done
  29.5 0.1 fusion.41
  29.6 0.7 fusion.39
  30.3 0.0 collective-permute-done
  30.3 1.8 %collective-permute-start.13 = (f32[528,128]{1,0:T(8,128)}, f32[528,128]{1,0:T(8,128)S(1)}, u32[]{:S(2)}, u32[]{:S(2)}) collective-permute-start(f32[528,128]{1,0:T(8,128)} %get-tuple-element.44), channel_id=1, source_target_pairs={{0,3},{1,2},{2,1},{3,0},{4,7},{5,6},{6,5},{7,4},{8,11},{9,10},{10,... | collective-permute-start | bytes 811016 | tf_op jit(solution)/shard_map/ppermute | solution.py:568
  32.1 5.0 %collective-permute-done.4 = f32[32,40,128]{2,1,0:T(8,128)S(1)} collective-permute-done((f32[32,40,128]{2,1,0:T(8,128)}, f32[32,40,128]{2,1,0:T(8,128)S(1)}, u32[]{:S(2)}, u32[]{:S(2)}) %collective-permute-start.4) | collective-permute-done | bytes 655392 | tf_op jit(solution)/shard_map/ppermute | solution.py:597
  37.2 1.5 %collective-permute-start.8 = (f32[528,128]{1,0:T(8,128)}, f32[528,128]{1,0:T(8,128)}, u32[]{:S(2)}, u32[]{:S(2)}) collective-permute-start(f32[528,128]{1,0:T(8,128)} %get-tuple-element.38), channel_id=1, source_target_pairs={{0,1},{1,0},{2,3},{3,2},{4,5},{5,4},{6,7},{7,6},{8,9},{9,8},{10,11... | collective-permute-start | bytes 811016 | tf_op jit(solution)/shard_map/ppermute | solution.py:568
  38.7 0.8 fusion.33.refs_18_.refs_10_
  39.5 0.0 collective-permute-done.10.refs_3_.refs_11_
  39.5 0.0 copy-start.4
  39.5 1.3 %collective-permute-start.9 = (f32[528,128]{1,0:T(8,128)}, f32[528,128]{1,0:T(8,128)}, u32[]{:S(2)}, u32[]{:S(2)}) collective-permute-start(f32[528,128]{1,0:T(8,128)} %get-tuple-element.39), channel_id=1, source_target_pairs={{0,2},{1,3},{2,0},{3,1},{4,6},{5,7},{6,4},{7,5},{8,10},{9,11},{10,... | collective-permute-start | bytes 811016 | tf_op jit(solution)/shard_map/ppermute | solution.py:568
  40.8 0.0 copy-done.3
  40.8 0.0 copy-done.2
  40.8 12.7 %top.1 = (f32[520,128]{1,0:T(8,128)}, f32[520,128]{1,0:T(8,128)}, f32[520,128]{1,0:T(8,128)}, f32[520,128]{1,0:T(8,128)}) custom-call(s32[1]{0:T(128)} %bitcast.me_ref, f32[32]{0:T(128)} %attenuation.13, f32[8,1024,128]{2,1,0:T(8,128)} %bitcast.19, f32[2,1024,128]{2,1,0:T(8,128)} %bitcast.23, s32[32,128]{1,0:T(8,128)} %refs_9_.3, f32[1280,128]{1,0:T(8,128)} %bitcast.27, ...), custom_call_target="tpu_custom_call" | custom-call | flops 15728640 | bytes 4194304 | tf_op jit(solution)/shard_map/top/pallas_call | solution.py:400
  53.5 0.0 collective-permute-done.11.refs_5_.refs_13_
  53.5 0.0 copy-start.5
  53.5 0.8 collective-permute-start.5
  54.3 0.1 compare_convert_fusion
  54.4 0.1 slice.138
  54.5 0.0 copy-done.1
  54.5 12.7 %bottom.1 = (f32[520,128]{1,0:T(8,128)}, f32[520,128]{1,0:T(8,128)}, f32[520,128]{1,0:T(8,128)}, f32[520,128]{1,0:T(8,128)}) custom-call(s32[1]{0:T(128)} %bitcast.me_ref, f32[32]{0:T(128)} %attenuation.13, f32[8,1024,128]{2,1,0:T(8,128)} %bitcast.20, f32[2,1024,128]{2,1,0:T(8,128)} %bitcast.24, s32[32,128]{1,0:T(8,128)} %refs_9_.3, f32[1280,128]{1,0:T(8,128)} %bitcast.25, ...), custom_call_target="tpu_custom_call" | custom-call | flops 15728640 | bytes 4194304 | tf_op jit(solution)/shard_map/bottom/pallas_call | solution.py:400
  67.1 0.0 copy-done.4
  67.2 0.0 collective-permute-done.12.refs_6_.refs_14_
  67.2 0.0 copy-start.6
  67.2 0.1 collective-permute-start.6
  67.3 0.0 collective-permute-done.13.refs_7_.refs_15_
  67.3 0.0 copy-start.7
  67.3 1.8 %collective-permute-start.7 = (f32[520,128]{1,0:T(8,128)}, f32[520,128]{1,0:T(8,128)S(1)}, u32[]{:S(2)}, u32[]{:S(2)}) collective-permute-start(f32[520,128]{1,0:T(8,128)} %get-tuple-element.36), channel_id=1, source_target_pairs={{0,3},{1,2},{2,1},{3,0},{4,7},{5,6},{6,5},{7,4},{8,11},{9,10},{10,... | collective-permute-start | bytes 798728 | tf_op jit(solution)/shard_map/ppermute | solution.py:568
  69.1 0.0 collective-permute-done.8.refs_1_.refs_9_
  69.1 0.1 collective-permute-start.1
  69.1 0.0 collective-permute-done.9.refs_2_.refs_10_
  69.1 0.1 collective-permute-start.2
  69.3 0.0 copy-done.5
  69.3 0.0 copy-done.6
  69.3 0.0 copy-done.7
  69.3 6.0 %react_inner.1 = (f32[32,8,32,128]{3,2,1,0:T(8,128)}, f32[8,32,128]{2,1,0:T(8,128)}) custom-call(s32[1]{0:T(128)} %bitcast.me_ref, s32[32]{0:T(128)} %consumed.5, f32[32]{0:T(128)} %attenuation.13, f32[32]{0:T(128)} %speeds.5, f32[528,128]{1,0:T(8,128)} %get-tuple-element.37.refs_0_.refs_8_, f32[528,128]{1,0:T(8,128)} %collective-permute-done.8.refs_1_.refs_9_, ...), custom_call_target="tpu_custom_call" | custom-call | flops 10485760 | bytes 4194304 | tf_op jit(solution)/shard_map/react_inner/pallas_call | solution.py:536
  75.2 1.1 %fusion.24 = f32[1,8,32,128]{3,2,1,0:T(8,128)S(1)} fusion(f32[8,32,128]{2,1,0:T(8,128)S(1)} %get-tuple-element.51, f32[8,1,128]{2,1,0:T(1,128)S(1)} %get-tuple-element.53, f32[8,1,128]{2,1,0:T(1,128)S(1)} %get-tuple-element.54, f32[8,32,128]{2,1,0:T(8,128)S(1)} %get-tuple-element.52, f32[8,34,128]{2,1,0:T(8,128)S(1)} %compare_convert_fusion, ...), kind=kLoop, calls=%fused_computation.34 | loop fusion | flops 851968 | bytes 1193472 | tf_op jit(solution)/shard_map/stack | solution.py:79
  76.4 0.0 collective-permute-done.5.refs_1_.refs_5_
  76.4 0.0 copy-start.8
  76.4 2.0 %collective-permute-start.3 = (f32[520,128]{1,0:T(8,128)}, f32[520,128]{1,0:T(8,128)S(1)}, u32[]{:S(2)}, u32[]{:S(2)}) collective-permute-start(f32[520,128]{1,0:T(8,128)} %get-tuple-element.31), channel_id=1, source_target_pairs={{0,3},{1,2},{2,1},{3,0},{4,7},{5,6},{6,5},{7,4},{8,11},{9,10},{10,... | collective-permute-start | bytes 798728 | tf_op jit(solution)/shard_map/ppermute | solution.py:568
  78.4 0.2 fusion.11
  78.6 0.7 pad_maximum_fusion
  79.3 0.0 collective-permute-done.6.refs_2_.refs_6_
  79.3 2.6 %collective-permute-done.7.refs_3_.refs_7_ = f32[520,128]{1,0:T(8,128)S(1)} collective-permute-done((f32[520,128]{1,0:T(8,128)}, f32[520,128]{1,0:T(8,128)S(1)}, u32[]{:S(2)}, u32[]{:S(2)}) %collective-permute-start.7) | collective-permute-done | bytes 266272 | tf_op jit(solution)/shard_map/ppermute | solution.py:568
  81.9 0.0 copy-done.11
  81.9 0.7 copy-done.12
  82.6 3.5 %react_top.1 = (f32[32,8,32,128]{3,2,1,0:T(8,128)}, f32[8,32,128]{2,1,0:T(8,128)}) custom-call(s32[1]{0:T(128)} %bitcast.me_ref, s32[32]{0:T(128)} %consumed.5, f32[32]{0:T(128)} %attenuation.13, f32[32]{0:T(128)} %speeds.5, f32[520,128]{1,0:T(8,128)} %get-tuple-element.33.refs_0_.refs_4_, ...), custom_call_target="tpu_custom_call", output_to_operand_aliasing={{0}: (15, {}), {1}: (16, {})} | custom-call | flops 5242880 | bytes 2097152 | tf_op jit(solution)/shard_map/react_top/pallas_call | solution.py:536
  86.1 0.0 collective-permute-done.1.refs_1_.refs_5_
  86.2 0.5 collective-permute-done.2.refs_2_.refs_6_
  86.6 6.0 %collective-permute-done.3.refs_3_.refs_7_ = f32[520,128]{1,0:T(8,128)S(1)} collective-permute-done((f32[520,128]{1,0:T(8,128)}, f32[520,128]{1,0:T(8,128)S(1)}, u32[]{:S(2)}, u32[]{:S(2)}) %collective-permute-start.3) | collective-permute-done | bytes 266272 | tf_op jit(solution)/shard_map/ppermute | solution.py:568
  92.7 0.0 copy-done.10
  92.7 0.7 copy-done.13
  93.4 3.5 %react_bottom.1 = (f32[32,8,32,128]{3,2,1,0:T(8,128)}, f32[8,32,128]{2,1,0:T(8,128)}) custom-call(s32[1]{0:T(128)} %bitcast.me_ref, s32[32]{0:T(128)} %consumed.5, f32[32]{0:T(128)} %attenuation.13, f32[32]{0:T(128)} %speeds.5, f32[520,128]{1,0:T(8,128)} %get-tuple-element.28.refs_0_.refs_4_, ...), custom_call_target="tpu_custom_call", output_to_operand_aliasing={{0}: (15, {}), {1}: (16, {})} | custom-call | flops 5242880 | bytes 2097152 | tf_op jit(solution)/shard_map/react_bottom/pallas_call | solution.py:536
  (17 shorter events, 0.1 us)
Async XLA Ops:
  4.4 25.9 %collective-permute-start = (f32[32,40,128]{2,1,0:T(8,128)}, f32[32,40,128]{2,1,0:T(8,128)S(1)}, u32[]{:S(2)}, u32[]{:S(2)}) collective-permute-start(f32[32,40,128]{2,1,0:T(8,128)} %get-tuple-element.27), channel_id=1, source_target_pairs={{4,0},{8,4},{12,8},{0,12},{5,1},{9,5},{13,9},{1,13},{6,2},{10,6},{... | collective-permute-start | bytes 1966088 | tf_op jit(solution)/shard_map/ppermute | solution.py:598
  8.6 28.6 %collective-permute-start.4 = (f32[32,40,128]{2,1,0:T(8,128)}, f32[32,40,128]{2,1,0:T(8,128)S(1)}, u32[]{:S(2)}, u32[]{:S(2)}) collective-permute-start(f32[32,40,128]{2,1,0:T(8,128)} %get-tuple-element.32), channel_id=1, source_target_pairs={{0,4},{4,8},{8,12},{12,0},{1,5},{5,9},{9,13},{13,1},{2,6},{6,10},{... | collective-permute-start | bytes 1966088 | tf_op jit(solution)/shard_map/ppermute | solution.py:597
  17.2 12.2 %copy-start = (f32[8,32,128]{2,1,0:T(8,128)S(1)}, f32[8,32,128]{2,1,0:T(8,128)}, u32[]{:S(2)}) copy-start(f32[8,32,128]{2,1,0:T(8,128)} %heat.1) | copy-start | bytes 393220
  17.2 23.5 %copy-start.3 = (s32[32,128]{1,0:T(8,128)S(1)}, s32[32,128]{1,0:T(8,128)}, u32[]{:S(2)}) copy-start(s32[32,128]{1,0:T(8,128)} %refs_9_.3) | copy-start | bytes 49156
  17.3 22.2 %collective-permute-start.10 = (f32[528,128]{1,0:T(8,128)}, f32[528,128]{1,0:T(8,128)S(1)}, u32[]{:S(2)}, u32[]{:S(2)}) collective-permute-start(f32[528,128]{1,0:T(8,128)} %get-tuple-element.40), channel_id=1, source_target_pairs={{0,3},{1,2},{2,1},{3,0},{4,7},{5,6},{6,5},{7,4},{8,11},{9,10},{10,... | collective-permute-start | bytes 811016 | tf_op jit(solution)/shard_map/ppermute | solution.py:568
  28.0 25.5 %collective-permute-start.11 = (f32[528,128]{1,0:T(8,128)}, f32[528,128]{1,0:T(8,128)S(1)}, u32[]{:S(2)}, u32[]{:S(2)}) collective-permute-start(f32[528,128]{1,0:T(8,128)} %get-tuple-element.42), channel_id=1, source_target_pairs={{0,1},{1,0},{2,3},{3,2},{4,5},{5,4},{6,7},{7,6},{8,9},{9,8},{10,11... | collective-permute-start | bytes 811016 | tf_op jit(solution)/shard_map/ppermute | solution.py:568
  28.1 39.1 %collective-permute-start.12 = (f32[528,128]{1,0:T(8,128)}, f32[528,128]{1,0:T(8,128)S(1)}, u32[]{:S(2)}, u32[]{:S(2)}) collective-permute-start(f32[528,128]{1,0:T(8,128)} %get-tuple-element.43), channel_id=1, source_target_pairs={{0,2},{1,3},{2,0},{3,1},{4,6},{5,7},{6,4},{7,5},{8,10},{9,11},{10,... | collective-permute-start | bytes 811016 | tf_op jit(solution)/shard_map/ppermute | solution.py:568
  30.3 24.2 %copy-start.1 = (f32[32,40,128]{2,1,0:T(8,128)}, f32[32,40,128]{2,1,0:T(8,128)S(1)}, u32[]{:S(2)}) copy-start(f32[32,40,128]{2,1,0:T(8,128)S(1)} %collective-permute-done) | copy-start | bytes 1966084
  30.3 37.0 %collective-permute-start.13 = (f32[528,128]{1,0:T(8,128)}, f32[528,128]{1,0:T(8,128)S(1)}, u32[]{:S(2)}, u32[]{:S(2)}) collective-permute-start(f32[528,128]{1,0:T(8,128)} %get-tuple-element.44), channel_id=1, source_target_pairs={{0,3},{1,2},{2,1},{3,0},{4,7},{5,6},{6,5},{7,4},{8,11},{9,10},{10,... | collective-permute-start | bytes 811016 | tf_op jit(solution)/shard_map/ppermute | solution.py:568
  37.1 3.6 %copy-start.2 = (f32[32,40,128]{2,1,0:T(8,128)}, f32[32,40,128]{2,1,0:T(8,128)S(1)}, u32[]{:S(2)}) copy-start(f32[32,40,128]{2,1,0:T(8,128)S(1)} %collective-permute-done.4) | copy-start | bytes 1966084
  37.2 31.9 %collective-permute-start.8 = (f32[528,128]{1,0:T(8,128)}, f32[528,128]{1,0:T(8,128)}, u32[]{:S(2)}, u32[]{:S(2)}) collective-permute-start(f32[528,128]{1,0:T(8,128)} %get-tuple-element.38), channel_id=1, source_target_pairs={{0,1},{1,0},{2,3},{3,2},{4,5},{5,4},{6,7},{7,6},{8,9},{9,8},{10,11... | collective-permute-start | bytes 811016 | tf_op jit(solution)/shard_map/ppermute | solution.py:568
  39.5 27.7 %copy-start.4 = (f32[528,128]{1,0:T(8,128)}, f32[528,128]{1,0:T(8,128)S(1)}, u32[]{:S(2)}) copy-start(f32[528,128]{1,0:T(8,128)S(1)} %collective-permute-done.10.refs_3_.refs_11_) | copy-start | bytes 811012
  39.5 29.6 %collective-permute-start.9 = (f32[528,128]{1,0:T(8,128)}, f32[528,128]{1,0:T(8,128)}, u32[]{:S(2)}, u32[]{:S(2)}) collective-permute-start(f32[528,128]{1,0:T(8,128)} %get-tuple-element.39), channel_id=1, source_target_pairs={{0,2},{1,3},{2,0},{3,1},{4,6},{5,7},{6,4},{7,5},{8,10},{9,11},{10,... | collective-permute-start | bytes 811016 | tf_op jit(solution)/shard_map/ppermute | solution.py:568
  53.5 15.8 %copy-start.5 = (f32[528,128]{1,0:T(8,128)}, f32[528,128]{1,0:T(8,128)S(1)}, u32[]{:S(2)}) copy-start(f32[528,128]{1,0:T(8,128)S(1)} %collective-permute-done.11.refs_5_.refs_13_) | copy-start | bytes 811012
  53.5 22.9 %collective-permute-start.5 = (f32[520,128]{1,0:T(8,128)}, f32[520,128]{1,0:T(8,128)S(1)}, u32[]{:S(2)}, u32[]{:S(2)}) collective-permute-start(f32[520,128]{1,0:T(8,128)} %get-tuple-element.34), channel_id=1, source_target_pairs={{0,1},{1,0},{2,3},{3,2},{4,5},{5,4},{6,7},{7,6},{8,9},{9,8},{10,11... | collective-permute-start | bytes 798728 | tf_op jit(solution)/shard_map/ppermute | solution.py:568
  67.2 2.1 %copy-start.6 = (f32[528,128]{1,0:T(8,128)}, f32[528,128]{1,0:T(8,128)S(1)}, u32[]{:S(2)}) copy-start(f32[528,128]{1,0:T(8,128)S(1)} %collective-permute-done.12.refs_6_.refs_14_) | copy-start | bytes 811012
  67.2 12.2 %collective-permute-start.6 = (f32[520,128]{1,0:T(8,128)}, f32[520,128]{1,0:T(8,128)S(1)}, u32[]{:S(2)}, u32[]{:S(2)}) collective-permute-start(f32[520,128]{1,0:T(8,128)} %get-tuple-element.35), channel_id=1, source_target_pairs={{0,2},{1,3},{2,0},{3,1},{4,6},{5,7},{6,4},{7,5},{8,10},{9,11},{10,... | collective-permute-start | bytes 798728 | tf_op jit(solution)/shard_map/ppermute | solution.py:568
  67.3 2.0 %copy-start.7 = (f32[528,128]{1,0:T(8,128)}, f32[528,128]{1,0:T(8,128)S(1)}, u32[]{:S(2)}) copy-start(f32[528,128]{1,0:T(8,128)S(1)} %collective-permute-done.13.refs_7_.refs_15_) | copy-start | bytes 811012
  67.3 14.6 %collective-permute-start.7 = (f32[520,128]{1,0:T(8,128)}, f32[520,128]{1,0:T(8,128)S(1)}, u32[]{:S(2)}, u32[]{:S(2)}) collective-permute-start(f32[520,128]{1,0:T(8,128)} %get-tuple-element.36), channel_id=1, source_target_pairs={{0,3},{1,2},{2,1},{3,0},{4,7},{5,6},{6,5},{7,4},{8,11},{9,10},{10,... | collective-permute-start | bytes 798728 | tf_op jit(solution)/shard_map/ppermute | solution.py:568
  69.1 17.1 %collective-permute-start.1 = (f32[520,128]{1,0:T(8,128)}, f32[520,128]{1,0:T(8,128)S(1)}, u32[]{:S(2)}, u32[]{:S(2)}) collective-permute-start(f32[520,128]{1,0:T(8,128)} %get-tuple-element.29), channel_id=1, source_target_pairs={{0,1},{1,0},{2,3},{3,2},{4,5},{5,4},{6,7},{7,6},{8,9},{9,8},{10,11... | collective-permute-start | bytes 798728 | tf_op jit(solution)/shard_map/ppermute | solution.py:568
  69.1 17.5 %collective-permute-start.2 = (f32[520,128]{1,0:T(8,128)}, f32[520,128]{1,0:T(8,128)S(1)}, u32[]{:S(2)}, u32[]{:S(2)}) collective-permute-start(f32[520,128]{1,0:T(8,128)} %get-tuple-element.30), channel_id=1, source_target_pairs={{0,2},{1,3},{2,0},{3,1},{4,6},{5,7},{6,4},{7,5},{8,10},{9,11},{10,... | collective-permute-start | bytes 798728 | tf_op jit(solution)/shard_map/ppermute | solution.py:568
  76.4 5.5 %copy-start.8 = (f32[520,128]{1,0:T(8,128)}, f32[520,128]{1,0:T(8,128)S(1)}, u32[]{:S(2)}) copy-start(f32[520,128]{1,0:T(8,128)S(1)} %collective-permute-done.5.refs_1_.refs_5_) | copy-start | bytes 798724
  76.4 16.3 %collective-permute-start.3 = (f32[520,128]{1,0:T(8,128)}, f32[520,128]{1,0:T(8,128)S(1)}, u32[]{:S(2)}, u32[]{:S(2)}) collective-permute-start(f32[520,128]{1,0:T(8,128)} %get-tuple-element.31), channel_id=1, source_target_pairs={{0,3},{1,2},{2,1},{3,0},{4,7},{5,6},{6,5},{7,4},{8,11},{9,10},{10,... | collective-permute-start | bytes 798728 | tf_op jit(solution)/shard_map/ppermute | solution.py:568
  79.3 2.6 %copy-start.11 = (f32[520,128]{1,0:T(8,128)}, f32[520,128]{1,0:T(8,128)S(1)}, u32[]{:S(2)}) copy-start(f32[520,128]{1,0:T(8,128)S(1)} %collective-permute-done.6.refs_2_.refs_6_) | copy-start | bytes 798724
  81.9 0.7 copy-start.12
  86.2 6.5 %copy-start.9 = (f32[520,128]{1,0:T(8,128)}, f32[520,128]{1,0:T(8,128)S(1)}, u32[]{:S(2)}) copy-start(f32[520,128]{1,0:T(8,128)S(1)} %collective-permute-done.1.refs_1_.refs_5_) | copy-start | bytes 798724
  86.6 6.1 %copy-start.10 = (f32[520,128]{1,0:T(8,128)}, f32[520,128]{1,0:T(8,128)S(1)}, u32[]{:S(2)}) copy-start(f32[520,128]{1,0:T(8,128)S(1)} %collective-permute-done.2.refs_2_.refs_6_) | copy-start | bytes 798724
  92.7 0.7 copy-start.13
